TPU v7x, 512 devices: a whole 4x8x8 slice. The times are simulated.
512 devices in a mesh: grp: 8 (over z), own: 64 (over y, x, core).
Axes of the slice: x: 4, y: 8, z: 8, core: 2. Of those that a mesh axis runs over, the one named last changes fastest.
Arguments:
- amps: bfloat16 [14336, 128, 128], P(('grp', 'own')), may hold values from -0.35 to 0.35, as said below
- ints: bfloat16 [14336, 128, 128], P(('grp', 'own')), may hold values from -0.5 to 0.5, as said below
- pno_energy: float32 [14336, 128], P(('grp', 'own')), may hold values from 0.2 to 2, as said below
- occ_energy: float32 [1000], replicated, may hold values from -1 to -0.2
- pair_occ: int32 [2, 14336], P(None, ('grp', 'own')), may hold values from 0 to 999, as said below
- mirror: int32 [14336], P(('grp', 'own')), may hold values from 0 to 14335, as said below
- edge_src: int32 [24576], P(('grp', 'own')), may hold values from 0 to 14335, as said below
- edge_dst: int32 [24576], P('grp'), may hold values from 0 to 14335, as said below
- edge_fock: float32 [24576], P(('grp', 'own')), may hold values from -6 to 6
- margin: bfloat16 [24576, 128, 128], P(('grp', 'own')), may hold values from -0.15 to 1.15
Outputs:
- residual: bfloat16 [14336, 128, 128], P(('grp', 'own'))
Inputs may be any that keep to these rules, and one draw needn't show every extreme that they name: `pair_occ`: each pair's two indices differ. The pair at mirror[p] has its two indices swapped. mirror is an involution without fixed points; a pair and its mirror lie in the same grp block of pairs but never on the same device; amps and ints of mirror[p] are the transposes of those of p, and pno_energy is equal. Of one device's pairs at most 1 have their mirror on any one other device, and that many do for some device. `edge_src`: every edge of a device has its source pair on that same device. `edge_dst`: an edge's target pair lies in the same group as its source, on another device; of one device's edges at most 1 end on pairs of any one other device, and at most 1 have the mirror of their target pair on any one device (that device itself included); both bounds are reached on some device. `amps`: mirror pairs hold transposed tiles. `ints`: mirror pairs hold transposed tiles. `pno_energy`: mirror pairs hold equal rows.
All inputs are finite; a program needn't handle non-finite values.
Results may differ from a plain program's by a relative error of at most 0.0065.
Values may be sent and summed in bfloat16 or wider, within the bound.
No kernel may reach another device: no remote copies, remote signals or barrier semaphores. Data moves between devices by JAX's collectives and lax.ppermute only.
A program may use at most 64 MiB of HBM per device.

v0:
```python
import jax
import jax.numpy as jnp
from jax import lax
from jax.sharding import PartitionSpec as P


def rank_within(targets, buckets):
    onehot = (targets[:, None] == lax.iota(jnp.int32, buckets)[None, :]).astype(jnp.int32)
    running = jnp.cumsum(onehot, axis=0)
    return jnp.sum(onehot * running, axis=1) - 1


def pick_rows(lookup, hit_mask):
    return jnp.sum(jnp.where(hit_mask, lookup[None, :], 0.0), axis=1)


def pack_tiles(tile_set, targets, owners, capacity):
    placed = targets * capacity + rank_within(targets, owners)
    blank_buffer = jnp.zeros((owners * capacity,) + tile_set.shape[1:], tile_set.dtype)
    return blank_buffer.at[placed].set(tile_set)


def arrival_sum(arrived, destination, row_ids, row_total, owners, capacity, my_owner):
    per_sender = destination.shape[0] // owners
    arriving = destination == my_owner
    sender = lax.iota(jnp.int32, owners * per_sender) // per_sender
    counted = (
        jnp.cumsum(arriving.reshape(owners, per_sender).astype(jnp.int32), axis=1).reshape(-1) - 1
    )
    column = sender * capacity + counted
    row_hit = (
        (row_ids[:, None] == lax.iota(jnp.int32, row_total)[None, :]) & arriving[:, None]
    ).astype(jnp.float32)
    column_hit = (column[:, None] == lax.iota(jnp.int32, owners * capacity)[None, :]).astype(
        jnp.float32
    )
    selector = jnp.dot(row_hit.T, column_hit).astype(jnp.bfloat16)
    tile_rows = arrived.shape[1]
    tile_cols = arrived.shape[2]
    summed = jnp.dot(
        selector,
        arrived.reshape(owners * capacity, tile_rows * tile_cols),
        preferred_element_type=jnp.float32,
    )
    return summed.reshape(row_total, tile_rows, tile_cols)


def local(
    amps, ints, pno_energy, occ_energy, pair_occ, mirror, edge_src, edge_dst, edge_fock, margin
):
    owners = lax.axis_size("own")
    my_owner = lax.axis_index("own")
    group_index = lax.axis_index("grp")
    per_device = amps.shape[0]
    pno_rank = amps.shape[1]
    edge_count = edge_src.shape[0]
    occ_count = occ_energy.shape[0]
    mirror_cap = (per_device + owners - 2) // (owners - 1)
    edge_cap = (edge_count + owners - 2) // (owners - 1)
    group_base = group_index * (owners * per_device)
    device_base = group_base + my_owner * per_device
    amp_f32 = amps.astype(jnp.float32)
    int_f32 = ints.astype(jnp.float32)
    pair_energy = jnp.sum((2.0 * int_f32 - jnp.swapaxes(int_f32, 1, 2)) * amp_f32, axis=(1, 2))
    occ_ids = lax.iota(jnp.int32, occ_count)
    first_hit = pair_occ[0][:, None] == occ_ids[None, :]
    second_hit = pair_occ[1][:, None] == occ_ids[None, :]
    partial_value = jnp.sum(jnp.where(first_hit, pair_energy[:, None], 0.0), axis=0)
    source_local = edge_src - device_base
    source_tiles = jnp.take(amps, source_local, axis=0)
    projected = jnp.einsum(
        "eab,ebc->eac", margin, source_tiles, preferred_element_type=jnp.float32
    ).astype(jnp.bfloat16)
    product = jnp.einsum("eab,ecb->eac", projected, margin, preferred_element_type=jnp.float32)
    coupled = (product * edge_fock[:, None, None]).astype(jnp.bfloat16)
    group_dst = edge_dst - group_base
    dst_owner = group_dst // per_device
    dst_slot = group_dst % per_device
    my_dst_owner = lax.dynamic_slice_in_dim(dst_owner, my_owner * edge_count, edge_count)
    mirror_local = mirror - group_base
    mirror_owner = mirror_local // per_device
    mirror_slot = mirror_local % per_device
    slot_ids = lax.iota(jnp.int32, per_device)
    same_owner = mirror_owner[:, None] == mirror_owner[None, :]
    out_rank = jnp.sum(same_owner & (slot_ids[None, :] < slot_ids[:, None]), axis=1)
    in_rank = jnp.sum(same_owner & (mirror_slot[None, :] < mirror_slot[:, None]), axis=1)
    out_place = mirror_owner * mirror_cap + out_rank
    in_place = mirror_owner * mirror_cap + in_rank
    outgoing = pack_tiles(coupled, my_dst_owner, owners, edge_cap)
    arrived = lax.all_to_all(outgoing, "own", split_axis=0, concat_axis=0, tiled=True)
    coupling = arrival_sum(arrived, dst_owner, dst_slot, per_device, owners, edge_cap, my_owner)
    occ_sums = lax.psum(partial_value, ("grp", "own"))
    cepa_shift = 0.5 * (pick_rows(occ_sums, first_hit) + pick_rows(occ_sums, second_hit))
    fock_pair = pick_rows(occ_energy, first_hit) + pick_rows(occ_energy, second_hit)
    diagonal = (
        pno_energy[:, :, None]
        + pno_energy[:, None, :]
        - fock_pair[:, None, None]
        - cepa_shift[:, None, None]
    )
    local_part = 0.5 * int_f32 + diagonal * amp_f32
    half_res = (local_part + coupling).astype(jnp.bfloat16)
    sent_tiles = (
        jnp.zeros((owners * mirror_cap, pno_rank, pno_rank), jnp.bfloat16)
        .at[out_place]
        .set(half_res)
    )
    returned = lax.all_to_all(sent_tiles, "own", split_axis=0, concat_axis=0, tiled=True)
    partner_tiles = jnp.swapaxes(jnp.take(returned, in_place, axis=0), 1, 2)
    return (half_res.astype(jnp.float32) + partner_tiles.astype(jnp.float32)).astype(jnp.bfloat16)


def solution(mesh):
    in_specs = (
        P(("grp", "own"), None, None),
        P(("grp", "own"), None, None),
        P(("grp", "own"), None),
        P(),
        P(None, ("grp", "own")),
        P(("grp", "own")),
        P(("grp", "own")),
        P("grp"),
        P(("grp", "own")),
        P(("grp", "own"), None, None),
    )
    out_specs = P(("grp", "own"), None, None)
    return jax.shard_map(local, mesh=mesh, in_specs=in_specs, out_specs=out_specs, check_vma=False)
```

profile of v0, /device:TPU:2, one launch (start us, length us, event | category | flops | bytes accessed | tf_op | source)
XLA Modules:
  0.0 255.8 jit_solution(17630321323486701804)
XLA Ops:
  0.0 0.0 copy-start
  0.0 0.0 copy-start.8
  0.0 0.8 fusion.33
  0.9 0.1 dynamic_slice.3
  0.9 0.1 fusion.25
  1.0 0.1 reduce_window_sum.23
  1.1 0.2 select_reduce_fusion.5
  1.3 0.1 compare_select_fusion.3
  1.4 0.7 compare_and_fusion.3
  2.0 3.1 %gather_fusion = bf16[48,128,128]{2,1,0:T(8,128)(2,1)} fusion(bf16[28,128,128]{2,1,0:T(8,128)(2,1)} %param.10, s32[1024]{0:T(1024)S(1)} %pad_clamp_fusion.1), kind=kCustom, calls=%fused_computation | custom fusion | bytes 3145920 | tf_op jit(solution)/shard_map/jit(_take)/gather | solution.py:70
  5.2 0.0 copy-done
  5.2 0.0 copy-done.8
  5.2 3.7 %multiply_convert_fusion = bf16[48,128,128]{2,1,0:T(8,128)(2,1)S(1)} fusion(bf16[48,128,128]{2,1,0:T(8,128)(2,1)S(1)} %copy-done, f32[48]{0:T(128)S(1)} %copy-done.8, bf16[48,128,128]{2,1,0:T(8,128)(2,1)} %gather_fusion, pred[48]{0:T(512)(128)(4,1)S(1)} %get-tuple-element.18), kind=kOutput, calls=%fused_computation.4 | convolution fusion | flops 405798912 | bytes 4718832 | tf_op jit(solution)/shard_map/eab,ecb->eac/dot_general | solution.py:74
  8.9 1.8 broadcast.97.clone
  10.7 6.6 %scatter_fusion = bf16[64,128,128]{2,1,0:T(8,128)(2,1)} fusion(bf16[64,128,128]{2,1,0:T(8,128)(2,1)} %broadcast.97.clone, s32[48]{0:T(128)S(1)} %compare_select_fusion.3, bf16[48,128,128]{2,1,0:T(8,128)(2,1)S(1)} %multiply_convert_fusion), kind=kCustom, calls=%fused_computation.2 | custom fusion | bytes 4718784 | tf_op jit(solution)/shard_map/scatter | solution.py:20
  17.3 0.0 copy-start.2
  17.3 11.0 %all-to-all-start = ((bf16[64,128,128]{2,1,0:T(8,128)(2,1)}), bf16[64,128,128]{2,1,0:T(8,128)(2,1)}, u32[]{:S(2)}, u32[]{:S(2)}) async-start(bf16[64,128,128]{2,1,0:T(8,128)(2,1)} %scatter_fusion), calls=%async_computation | async-start | bytes 4194304 | tf_op jit(solution)/shard_map/all_to_all | solution.py:90
  28.3 0.0 copy-done.2
  28.3 1.3 copy.39
  29.6 0.0 copy-start.6
  29.6 0.1 reshape.67
  29.6 0.2 reduce_window_sum.22
  29.9 0.1 sub.71
  30.0 1.5 copy.37
  31.4 0.0 copy-done.6
  31.4 0.0 copy-start.5
  31.5 0.0 copy-start.7
  31.5 0.0 copy-start.4
  31.5 2.0 fusion.3
  33.5 0.1 select_reduce_fusion.2
  33.6 137.7 %psum.7 = f32[1000]{0:T(1024)S(1)} all-reduce(f32[1000]{0:T(1024)S(1)} %select_reduce_fusion.2), channel_id=1, replica_groups=mesh['grp'=8,'own'=64] {'grp','own'}, use_global_device_ids=true, to_apply=%region_4.5 | all-reduce | flops 1000 | bytes 8000 | tf_op jit(solution)/shard_map/psum | solution.py:92
  171.3 0.0 copy-done.5
  171.3 0.3 select_reduce_fusion
  171.6 0.0 copy-done.7
  171.6 0.2 convert_reduce_fusion.1
  171.8 0.0 copy-done.4
  171.9 0.0 all-to-all-done
  171.9 4.9 %fusion = f32[28,128,128]{2,0,1:T(8,128)} fusion(s32[3072]{0:T(1024)S(1)} %get-tuple-element.25, s32[3072]{0:T(1024)S(1)} %get-tuple-element.24, pred[3072]{0:T(1024)(128)(4,1)S(1)} %get-tuple-element.16, bf16[8,8,128,128]{3,2,1,0:T(8,128)(2,1)} %bitcast.8), kind=kOutput, calls=%fused_computation.8 | convolution fusion | flops 70100736 | bytes 3959808 | tf_op jit(solution)/shard_map/dot_general | solution.py:40
  176.8 0.0 copy-start.3
  176.8 2.9 %copy.43 = f32[28,128,128]{1,2,0:T(8,128)} copy(f32[28,128,128]{2,0,1:T(8,128)} %fusion) | data formatting | bytes 3670016 | tf_op jit(solution)/shard_map/dot_general | solution.py:40
  179.7 0.0 copy-done.3
  179.7 3.1 %fusion.6 = bf16[28,128,128]{1,2,0:T(8,128)(2,1)} fusion(f32[28,128,128]{1,2,0:T(8,128)} %copy.43, bf16[28,128,128]{1,2,0:T(8,128)(2,1)} %copy.39, f32[28,128,128]{1,2,0:T(8,128)S(1)} %copy.37, f32[28]{0:T(128)S(1)} %add_multiply_fusion, f32[28]{0:T(128)S(1)} %add.110, f32[28,128]{1,0:T(8,128)S(1)} %copy-done.3), kind=kLoop, calls=%fused_computation.14 | loop fusion | flops 4128768 | bytes 5519584 | tf_op jit(solution)/shard_map/convert_element_type | solution.py:102
  182.8 1.6 copy.44
  184.4 1.8 broadcast.97
  186.2 4.5 %scatter_fusion.1 = bf16[64,128,128]{2,1,0:T(8,128)(2,1)} fusion(bf16[64,128,128]{2,1,0:T(8,128)(2,1)} %broadcast.97, s32[28]{0:T(128)S(1)} %compare_select_fusion, bf16[28,128,128]{2,1,0:T(8,128)(2,1)S(1)} %copy.44), kind=kCustom, calls=%fused_computation.3 | custom fusion | bytes 2752624 | tf_op jit(solution)/shard_map/scatter | solution.py:106
  190.7 7.8 %all-to-all-start.1 = ((bf16[64,128,128]{2,1,0:T(8,128)(2,1)}), bf16[64,128,128]{2,1,0:T(8,128)(2,1)}, u32[]{:S(2)}, u32[]{:S(2)}) async-start(bf16[64,128,128]{2,1,0:T(8,128)(2,1)} %scatter_fusion.1), calls=%async_computation.1 | async-start | bytes 4194304 | tf_op jit(solution)/shard_map/all_to_all | solution.py:108
  198.5 0.0 copy-start.1
  198.6 51.1 %all-to-all-done.1 = bf16[64,128,128]{2,1,0:T(8,128)(2,1)} async-done(((bf16[64,128,128]{2,1,0:T(8,128)(2,1)}), bf16[64,128,128]{2,1,0:T(8,128)(2,1)}, u32[]{:S(2)}, u32[]{:S(2)}) %all-to-all-start.1) | async-done | bytes 2097184 | tf_op jit(solution)/shard_map/all_to_all | solution.py:108
  249.7 3.2 %gather_fusion.1 = bf16[28,128,128]{2,1,0:T(8,128)(2,1)} fusion(bf16[64,128,128]{2,1,0:T(8,128)(2,1)} %all-to-all-done.1, s32[1024]{0:T(1024)S(1)} %pad_clamp_fusion), kind=kCustom, calls=%fused_computation.1 | custom fusion | bytes 1835120 | tf_op jit(solution)/shard_map/jit(_take)/gather | solution.py:109
  252.9 0.0 copy-done.1
  252.9 1.6 fusion.7
  254.5 1.3 copy.45
  (10 shorter events, 0.1 us)
Async XLA Ops:
  0.0 5.2 %copy-start = (bf16[48,128,128]{2,1,0:T(8,128)(2,1)S(1)}, bf16[48,128,128]{2,1,0:T(8,128)(2,1)}, u32[]{:S(2)}) copy-start(bf16[48,128,128]{2,1,0:T(8,128)(2,1)} %param.19) | copy-start | bytes 4718596
  0.0 5.2 %copy-start.8 = (f32[48]{0:T(128)S(1)}, f32[48]{0:T(128)}, u32[]{:S(2)}) copy-start(f32[48]{0:T(128)} %param.18) | copy-start | bytes 580
  17.3 11.0 %copy-start.2 = (bf16[28,128,128]{2,1,0:T(8,128)(2,1)S(1)}, bf16[28,128,128]{2,1,0:T(8,128)(2,1)}, u32[]{:S(2)}) copy-start(bf16[28,128,128]{2,1,0:T(8,128)(2,1)} %param.10) | copy-start | bytes 2752516
  17.3 154.6 %all-to-all-start = ((bf16[64,128,128]{2,1,0:T(8,128)(2,1)}), bf16[64,128,128]{2,1,0:T(8,128)(2,1)}, u32[]{:S(2)}, u32[]{:S(2)}) async-start(bf16[64,128,128]{2,1,0:T(8,128)(2,1)} %scatter_fusion), calls=%async_computation | async-start | bytes 4194304 | tf_op jit(solution)/shard_map/all_to_all | solution.py:90
  29.6 1.8 copy-start.6
  31.4 139.9 %copy-start.5 = (f32[1000]{0:T(1024)S(1)}, f32[1000]{0:T(1024)}, u32[]{:S(2)}) copy-start(f32[1000]{0:T(1024)} %param.13) | copy-start | bytes 12004
  31.5 140.2 %copy-start.7 = (s32[28]{0:T(128)S(1)}, s32[28]{0:T(128)}, u32[]{:S(2)}) copy-start(s32[28]{0:T(128)} %param.15) | copy-start | bytes 340
  31.5 140.4 %copy-start.4 = (s32[3072]{0:T(1024)S(1)}, s32[3072]{0:T(1024)}, u32[]{:S(2)}) copy-start(s32[3072]{0:T(1024)} %param.17) | copy-start | bytes 36868
  176.8 2.9 %copy-start.3 = (f32[28,128]{1,0:T(8,128)S(1)}, f32[28,128]{1,0:T(8,128)}, u32[]{:S(2)}) copy-start(f32[28,128]{1,0:T(8,128)} %param.12) | copy-start | bytes 43012
  190.7 59.0 %all-to-all-start.1 = ((bf16[64,128,128]{2,1,0:T(8,128)(2,1)}), bf16[64,128,128]{2,1,0:T(8,128)(2,1)}, u32[]{:S(2)}, u32[]{:S(2)}) async-start(bf16[64,128,128]{2,1,0:T(8,128)(2,1)} %scatter_fusion.1), calls=%async_computation.1 | async-start | bytes 4194304 | tf_op jit(solution)/shard_map/all_to_all | solution.py:108
  198.5 54.4 %copy-start.1 = (bf16[28,128,128]{1,2,0:T(8,128)(2,1)S(1)}, bf16[28,128,128]{1,2,0:T(8,128)(2,1)}, u32[]{:S(2)}) copy-start(bf16[28,128,128]{1,2,0:T(8,128)(2,1)} %fusion.6) | copy-start | bytes 2752516
where the time goes:
time: 257 us; the launch traced here: 256 us
  blocking collectives  138 us (54%)
  waiting for transfers between devices  51.1 us (20%)
  local copies, waits for them, and re-layouts  29.9 us (12%)
  starting transfers between devices  18.8 us (7%)
  other arithmetic  9.49 us (4%)
  matrix products  8.65 us (3%)
    psum x1, blocking collectives, local(): occ_sums = lax.psum(partial_value, ('grp', 'own'))  138 us
    all_to_all x1, waiting for transfers between devices, local(): lax.all_to_all(sent_tiles, 'own', split_axis=0, concat_axis=0, tiled=True)  51.1 us
    all_to_all x1, starting transfers between devices, local(): lax.all_to_all(outgoing, 'own', split_axis=0, concat_axis=0, tiled=True)  11 us
    all_to_all x1, starting transfers between devices, local(): lax.all_to_all(sent_tiles, 'own', split_axis=0, concat_axis=0, tiled=True)  7.79 us
    scatter x1, local copies, waits for them, and re-layouts, pack_tiles(): return blank_buffer.at[placed].set(tile_set)  6.61 us
  transfers between devices with their start and end apart: 2, of which 1 were waited for; matrix products, arithmetic and copies ran while one was open for 2% of the time, Pallas kernels for 0%

commit v1 on v0

--- a/solution.py
+++ b/solution.py
@@ -89,7 +89,9 @@
     outgoing = pack_tiles(coupled, my_dst_owner, owners, edge_cap)
     arrived = lax.all_to_all(outgoing, "own", split_axis=0, concat_axis=0, tiled=True)
     coupling = arrival_sum(arrived, dst_owner, dst_slot, per_device, owners, edge_cap, my_owner)
-    occ_sums = lax.psum(partial_value, ("grp", "own"))
+    occ_sums = partial_value
+    for j in ("own", "grp"):
+        occ_sums = lax.psum(occ_sums, axis_name=j)
     cepa_shift = 0.5 * (pick_rows(occ_sums, first_hit) + pick_rows(occ_sums, second_hit))
     fock_pair = pick_rows(occ_energy, first_hit) + pick_rows(occ_energy, second_hit)
     diagonal = (

time: 257 us -> 304 us (1.18)
  blocking collectives: 138 us -> 178 us
  starting transfers between devices: 18.8 us -> 25.6 us
    psum x1 -> x2, blocking collectives: 138 us -> 178 us  [local(): occ_sums = lax.psum(occ_sums, axis_name=j)]
    all_to_all x1, starting transfers between devices: 7.79 us -> 14.7 us  [local(): lax.all_to_all(sent_tiles, 'own', split_axis=0, concat_axis=0, tiled=True)]
where the time goes in v1:
time: 304 us; the launch traced here: 303 us
  blocking collectives  178 us (59%)
  waiting for transfers between devices  51.1 us (17%)
  local copies, waits for them, and re-layouts  29.9 us (10%)
  starting transfers between devices  25.6 us (8%)
  other arithmetic  9.49 us (3%)
  matrix products  8.65 us (3%)
    psum x2, blocking collectives, local(): occ_sums = lax.psum(occ_sums, axis_name=j)  178 us
    all_to_all x1, waiting for transfers between devices, local(): lax.all_to_all(sent_tiles, 'own', split_axis=0, concat_axis=0, tiled=True)  51.1 us
    all_to_all x1, starting transfers between devices, local(): lax.all_to_all(sent_tiles, 'own', split_axis=0, concat_axis=0, tiled=True)  14.7 us
    all_to_all x1, starting transfers between devices, local(): lax.all_to_all(outgoing, 'own', split_axis=0, concat_axis=0, tiled=True)  11 us
    scatter x1, local copies, waits for them, and re-layouts, pack_tiles(): return blank_buffer.at[placed].set(tile_set)  6.61 us
  transfers between devices with their start and end apart: 2, of which 1 were waited for; matrix products, arithmetic and copies ran while one was open for 2% of the time, Pallas kernels for 0%

profile of v1, /device:TPU:2, one launch (start us, length us, event | category | flops | bytes accessed | tf_op | source)
XLA Modules:
  0.0 302.8 jit_solution(12922482726758945807)
XLA Ops:
  0.0 0.0 copy-start
  0.0 0.0 copy-start.8
  0.0 0.8 fusion.33
  0.9 0.1 dynamic_slice.3
  0.9 0.1 fusion.25
  1.0 0.1 reduce_window_sum.23
  1.1 0.2 select_reduce_fusion.5
  1.3 0.1 compare_select_fusion.3
  1.4 0.7 compare_and_fusion.3
  2.0 3.1 %gather_fusion = bf16[48,128,128]{2,1,0:T(8,128)(2,1)} fusion(bf16[28,128,128]{2,1,0:T(8,128)(2,1)} %param.10, s32[1024]{0:T(1024)S(1)} %pad_clamp_fusion.1), kind=kCustom, calls=%fused_computation | custom fusion | bytes 3145920 | tf_op jit(solution)/shard_map/jit(_take)/gather | solution.py:70
  5.2 0.0 copy-done
  5.2 0.0 copy-done.8
  5.2 3.7 %multiply_convert_fusion = bf16[48,128,128]{2,1,0:T(8,128)(2,1)S(1)} fusion(bf16[48,128,128]{2,1,0:T(8,128)(2,1)S(1)} %copy-done, f32[48]{0:T(128)S(1)} %copy-done.8, bf16[48,128,128]{2,1,0:T(8,128)(2,1)} %gather_fusion, pred[48]{0:T(512)(128)(4,1)S(1)} %get-tuple-element.18), kind=kOutput, calls=%fused_computation.4 | convolution fusion | flops 405798912 | bytes 4718832 | tf_op jit(solution)/shard_map/eab,ecb->eac/dot_general | solution.py:74
  8.9 1.8 broadcast.97.clone
  10.7 6.6 %scatter_fusion = bf16[64,128,128]{2,1,0:T(8,128)(2,1)} fusion(bf16[64,128,128]{2,1,0:T(8,128)(2,1)} %broadcast.97.clone, s32[48]{0:T(128)S(1)} %compare_select_fusion.3, bf16[48,128,128]{2,1,0:T(8,128)(2,1)S(1)} %multiply_convert_fusion), kind=kCustom, calls=%fused_computation.2 | custom fusion | bytes 4718784 | tf_op jit(solution)/shard_map/scatter | solution.py:20
  17.3 0.0 copy-start.2
  17.3 11.0 %all-to-all-start = ((bf16[64,128,128]{2,1,0:T(8,128)(2,1)}), bf16[64,128,128]{2,1,0:T(8,128)(2,1)}, u32[]{:S(2)}, u32[]{:S(2)}) async-start(bf16[64,128,128]{2,1,0:T(8,128)(2,1)} %scatter_fusion), calls=%async_computation | async-start | bytes 4194304 | tf_op jit(solution)/shard_map/all_to_all | solution.py:90
  28.3 0.0 copy-done.2
  28.3 1.3 copy.39
  29.6 0.0 copy-start.6
  29.6 0.1 reshape.67
  29.6 0.2 reduce_window_sum.22
  29.9 0.1 sub.71
  30.0 1.5 copy.37
  31.4 0.0 copy-done.6
  31.4 0.0 copy-start.5
  31.5 0.0 copy-start.7
  31.5 0.0 copy-start.4
  31.5 2.0 fusion.3
  33.5 0.1 select_reduce_fusion.2
  33.6 154.6 %psum.14 = f32[1000]{0:T(1024)S(1)} all-reduce(f32[1000]{0:T(1024)S(1)} %select_reduce_fusion.2), channel_id=1, replica_groups=mesh['grp'=8,'own'=64] {'own'}, use_global_device_ids=true, to_apply=%region_4.5 | all-reduce | flops 1000 | bytes 8000 | tf_op jit(solution)/shard_map/psum | solution.py:94
  188.2 23.2 %psum.15 = f32[1000]{0:T(1024)S(1)} all-reduce(f32[1000]{0:T(1024)S(1)} %psum.14), channel_id=1, replica_groups=mesh['grp'=8,'own'=64] {'grp'}, use_global_device_ids=true, to_apply=%region_5.6 | all-reduce | flops 1000 | bytes 8000 | tf_op jit(solution)/shard_map/psum | solution.py:94
  211.4 0.0 copy-done.5
  211.4 0.3 select_reduce_fusion
  211.7 0.0 copy-done.7
  211.7 0.2 convert_reduce_fusion.1
  212.0 0.0 copy-done.4
  212.0 0.0 all-to-all-done
  212.0 4.9 %fusion = f32[28,128,128]{2,0,1:T(8,128)} fusion(s32[3072]{0:T(1024)S(1)} %get-tuple-element.25, s32[3072]{0:T(1024)S(1)} %get-tuple-element.24, pred[3072]{0:T(1024)(128)(4,1)S(1)} %get-tuple-element.16, bf16[8,8,128,128]{3,2,1,0:T(8,128)(2,1)} %bitcast.8), kind=kOutput, calls=%fused_computation.8 | convolution fusion | flops 70100736 | bytes 3959808 | tf_op jit(solution)/shard_map/dot_general | solution.py:40
  216.9 0.0 copy-start.3
  216.9 2.9 copy.43
  219.9 0.0 copy-done.3
  219.9 3.1 %fusion.6 = bf16[28,128,128]{1,2,0:T(8,128)(2,1)} fusion(f32[28,128,128]{1,2,0:T(8,128)} %copy.43, bf16[28,128,128]{1,2,0:T(8,128)(2,1)} %copy.39, f32[28,128,128]{1,2,0:T(8,128)S(1)} %copy.37, f32[28]{0:T(128)S(1)} %add_multiply_fusion, f32[28]{0:T(128)S(1)} %add.112, f32[28,128]{1,0:T(8,128)S(1)} %copy-done.3), kind=kLoop, calls=%fused_computation.14 | loop fusion | flops 4128768 | bytes 5519584 | tf_op jit(solution)/shard_map/convert_element_type | solution.py:104
  222.9 1.6 copy.44
  224.5 1.8 broadcast.97
  226.3 4.5 %scatter_fusion.1 = bf16[64,128,128]{2,1,0:T(8,128)(2,1)} fusion(bf16[64,128,128]{2,1,0:T(8,128)(2,1)} %broadcast.97, s32[28]{0:T(128)S(1)} %compare_select_fusion, bf16[28,128,128]{2,1,0:T(8,128)(2,1)S(1)} %copy.44), kind=kCustom, calls=%fused_computation.3 | custom fusion | bytes 2752624 | tf_op jit(solution)/shard_map/scatter | solution.py:108
  230.8 14.7 %all-to-all-start.1 = ((bf16[64,128,128]{2,1,0:T(8,128)(2,1)}), bf16[64,128,128]{2,1,0:T(8,128)(2,1)}, u32[]{:S(2)}, u32[]{:S(2)}) async-start(bf16[64,128,128]{2,1,0:T(8,128)(2,1)} %scatter_fusion.1), calls=%async_computation.1 | async-start | bytes 4194304 | tf_op jit(solution)/shard_map/all_to_all | solution.py:110
  245.5 0.0 copy-start.1
  245.5 51.1 %all-to-all-done.1 = bf16[64,128,128]{2,1,0:T(8,128)(2,1)} async-done(((bf16[64,128,128]{2,1,0:T(8,128)(2,1)}), bf16[64,128,128]{2,1,0:T(8,128)(2,1)}, u32[]{:S(2)}, u32[]{:S(2)}) %all-to-all-start.1) | async-done | bytes 2097184 | tf_op jit(solution)/shard_map/all_to_all | solution.py:110
  296.7 3.2 %gather_fusion.1 = bf16[28,128,128]{2,1,0:T(8,128)(2,1)} fusion(bf16[64,128,128]{2,1,0:T(8,128)(2,1)} %all-to-all-done.1, s32[1024]{0:T(1024)S(1)} %pad_clamp_fusion), kind=kCustom, calls=%fused_computation.1 | custom fusion | bytes 1835120 | tf_op jit(solution)/shard_map/jit(_take)/gather | solution.py:111
  299.9 0.0 copy-done.1
  299.9 1.6 fusion.7
  301.5 1.3 copy.45
  (10 shorter events, 0.1 us)
Async XLA Ops:
  0.0 5.2 %copy-start = (bf16[48,128,128]{2,1,0:T(8,128)(2,1)S(1)}, bf16[48,128,128]{2,1,0:T(8,128)(2,1)}, u32[]{:S(2)}) copy-start(bf16[48,128,128]{2,1,0:T(8,128)(2,1)} %param.19) | copy-start | bytes 4718596
  0.0 5.2 %copy-start.8 = (f32[48]{0:T(128)S(1)}, f32[48]{0:T(128)}, u32[]{:S(2)}) copy-start(f32[48]{0:T(128)} %param.18) | copy-start | bytes 580
  17.3 11.0 %copy-start.2 = (bf16[28,128,128]{2,1,0:T(8,128)(2,1)S(1)}, bf16[28,128,128]{2,1,0:T(8,128)(2,1)}, u32[]{:S(2)}) copy-start(bf16[28,128,128]{2,1,0:T(8,128)(2,1)} %param.10) | copy-start | bytes 2752516
  17.3 194.7 %all-to-all-start = ((bf16[64,128,128]{2,1,0:T(8,128)(2,1)}), bf16[64,128,128]{2,1,0:T(8,128)(2,1)}, u32[]{:S(2)}, u32[]{:S(2)}) async-start(bf16[64,128,128]{2,1,0:T(8,128)(2,1)} %scatter_fusion), calls=%async_computation | async-start | bytes 4194304 | tf_op jit(solution)/shard_map/all_to_all | solution.py:90
  29.6 1.8 copy-start.6
  31.4 180.0 %copy-start.5 = (f32[1000]{0:T(1024)S(1)}, f32[1000]{0:T(1024)}, u32[]{:S(2)}) copy-start(f32[1000]{0:T(1024)} %param.13) | copy-start | bytes 12004
  31.5 180.3 %copy-start.7 = (s32[28]{0:T(128)S(1)}, s32[28]{0:T(128)}, u32[]{:S(2)}) copy-start(s32[28]{0:T(128)} %param.15) | copy-start | bytes 340
  31.5 180.5 %copy-start.4 = (s32[3072]{0:T(1024)S(1)}, s32[3072]{0:T(1024)}, u32[]{:S(2)}) copy-start(s32[3072]{0:T(1024)} %param.17) | copy-start | bytes 36868
  216.9 2.9 copy-start.3
  230.8 65.8 %all-to-all-start.1 = ((bf16[64,128,128]{2,1,0:T(8,128)(2,1)}), bf16[64,128,128]{2,1,0:T(8,128)(2,1)}, u32[]{:S(2)}, u32[]{:S(2)}) async-start(bf16[64,128,128]{2,1,0:T(8,128)(2,1)} %scatter_fusion.1), calls=%async_computation.1 | async-start | bytes 4194304 | tf_op jit(solution)/shard_map/all_to_all | solution.py:110
  245.5 54.4 %copy-start.1 = (bf16[28,128,128]{1,2,0:T(8,128)(2,1)S(1)}, bf16[28,128,128]{1,2,0:T(8,128)(2,1)}, u32[]{:S(2)}) copy-start(bf16[28,128,128]{1,2,0:T(8,128)(2,1)} %fusion.6) | copy-start | bytes 2752516
